TPU v7x, 512 devices: a whole 4x8x8 slice. The times are simulated.
512 devices in a mesh: row: 16 (over z, y_lo), col: 32 (over x, y_hi, core).
Axes of the slice: x: 4, y: 8 (y_hi: 4, y_lo: 2; y = y_hi * 2 + y_lo), z: 8, core: 2. Of those that a mesh axis runs over, the one named last changes fastest.
Arguments:
- features: bfloat16 [65536, 128], P(('col', 'row')), may hold values from -6 to 6
- grad_out: bfloat16 [65536, 128], P(('row', 'col')), may hold values from -6 to 6
- weight: bfloat16 [128, 128], replicated, may hold values from -0.5 to 0.5
- block_ids: int32 [16, 32, 152], P('row', 'col'), may hold values from 0 to 511, as said below
- block_vals: bfloat16 [16, 32, 152, 128, 128], P('row', 'col'), may hold values from -0.0390625 to 0.0390625
- block_count: int32 [16, 32], P('row', 'col'), may hold values from 1 to 152
- node_perm: int32 [512, 128], P(('col', 'row')), may hold values from 0 to 127, each once within a row
Outputs:
- feature_grad: bfloat16 [65536, 128], P(('col', 'row'))
- weight_grad: float32 [128, 128], replicated
Inputs may be any that keep to these rules, and one draw needn't show every extreme that they name: `block_ids`: in each tile the 152 entries are distinct block positions p * 16 + q; slots at or beyond block_count are empty and must be ignored. `node_perm`: each row is a permutation of 0 to 127.
All inputs are finite; a program needn't handle non-finite values.
Results may differ from a plain program's by a relative error of at most 0.0059.
Values may be sent and summed in bfloat16 or wider, within the bound.
A program may use at most 128 MiB of HBM per device.

v0:
```python
import math
import jax
import jax.numpy as jnp
from jax import lax
from jax.sharding import PartitionSpec as P

BLOCK = 128


def grad_step(agg_low, grad_rows, weight):
    pre = jnp.dot(agg_low, weight, preferred_element_type=jnp.float32)
    sigma = jax.nn.sigmoid(pre)
    grad_pre = (grad_rows.astype(jnp.float32) * sigma * (1.0 + pre * (1.0 - sigma))).astype(
        jnp.bfloat16
    )
    grad_agg = lax.dot_general(
        grad_pre, weight, (((1,), (1,)), ((), ())), preferred_element_type=jnp.float32
    )
    return (grad_pre, grad_agg.astype(jnp.bfloat16))


def block_sums(product, targets, live, segments):
    routed = jnp.where(live, targets, segments)
    summed = jax.ops.segment_sum(product, routed, num_segments=segments + 1)
    return summed[:segments]


def shards(features, grad_out, weight, block_ids, block_vals, block_count, node_perm):
    nodes_dev = grad_out.shape[0]
    hidden = weight.shape[0]
    tile_ids = block_ids[0, 0]
    values = block_vals[0, 0]
    count_live = block_count[0, 0]
    slots_tile = tile_ids.shape[0]
    row_count = nodes_dev * lax.axis_size("col") // BLOCK
    col_count = nodes_dev * lax.axis_size("row") // BLOCK
    total_nodes = nodes_dev * lax.axis_size("row") * lax.axis_size("col")
    live = jnp.arange(slots_tile, dtype=jnp.int32) < count_live
    block_row = tile_ids // col_count
    block_col = tile_ids % col_count
    column_source = lax.all_gather(features, "row", axis=0, tiled=True)
    picked = column_source.reshape(col_count, BLOCK, hidden)[block_col]
    product = jnp.einsum("kij,kjf->kif", values, picked, preferred_element_type=jnp.float32)
    partial_value = block_sums(product, block_row, live, row_count).reshape(
        row_count * BLOCK, hidden
    )
    aggregate = lax.psum_scatter(partial_value, "col", scatter_dimension=0, tiled=True)
    agg_low = aggregate.astype(jnp.bfloat16)
    grad_pre, grad_share = grad_step(agg_low, grad_out, weight)
    weight_part = jnp.dot(agg_low.T, grad_pre, preferred_element_type=jnp.float32)
    grad_rows = lax.all_gather(grad_share, "col", axis=0, tiled=True)
    weight_grad = lax.psum(weight_part, ("row", "col")) * (1.0 / math.sqrt(total_nodes))
    picked_back = grad_rows.reshape(row_count, BLOCK, hidden)[block_row]
    product_back = jnp.einsum(
        "kij,kif->kjf", values, picked_back, preferred_element_type=jnp.float32
    )
    partial_back = block_sums(product_back, block_col, live, col_count).reshape(
        col_count * BLOCK, hidden
    )
    grad_share_cols = lax.psum_scatter(partial_back, "row", scatter_dimension=0, tiled=True)
    rounded = grad_share_cols.astype(jnp.bfloat16)
    feature_grad = rounded[node_perm[0]]
    return (feature_grad, weight_grad)


def solution(mesh):
    in_specs = (
        P(("col", "row"), None),
        P(("row", "col"), None),
        P(),
        P("row", "col", None),
        P("row", "col", None, None, None),
        P("row", "col"),
        P(("col", "row"), None),
    )
    out_specs = (P(("col", "row"), None), P())
    return jax.shard_map(shards, mesh=mesh, in_specs=in_specs, out_specs=out_specs, check_vma=False)
```

profile of v0, /device:TPU:4, one launch (start us, length us, event | category | flops | bytes accessed | tf_op | source)
XLA Modules:
  0.0 607.2 jit_solution(2033896433721760579)
XLA Ops:
  7.2 0.0 reduce-scatter.3.cloned.1.call-start
  7.2 0.7 compare_select_fusion
  8.6 44.5 %all_gather.6 = bf16[2048,128]{1,0:T(8,128)(2,1)S(1)} all-gather(bf16[128,128]{1,0:T(8,128)(2,1)} %param.7), channel_id=1, replica_groups=mesh['row'=16,'col'=32] {'row'}, dimensions={0}, use_global_device_ids=true | all-gather | bytes 557056 | tf_op jit(solution)/shard_map/all_gather | solution.py:41
  53.1 7.7 %gather_fusion = bf16[152,128,128]{2,1,0:T(8,128)(2,1)} fusion(bf16[16,128,128]{2,1,0:T(8,128)(2,1)S(1)} %bitcast.46, s32[1024]{0:T(1024)S(1)} %pad_clamp_fusion.2), kind=kCustom, calls=%fused_computation | custom fusion | bytes 9962080 | tf_op jit(solution)/shard_map/gather | solution.py:42
  60.8 11.3 %fusion.4 = f32[152,128,128]{1,2,0:T(8,128)} fusion(bf16[152,128,128]{2,1,0:T(8,128)(2,1)} %gather_fusion, bf16[1,1,152,128,128]{4,3,2,1,0:T(8,128)(2,1)} %param.11), kind=kOutput, calls=%fused_computation.9 | convolution fusion | flops 637534208 | bytes 19922944 | tf_op jit(solution)/shard_map/kij,kjf->kif/dot_general | solution.py:43
  72.1 11.3 %copy.12 = f32[152,128,128]{2,1,0:T(8,128)} copy(f32[152,128,128]{1,2,0:T(8,128)} %fusion.4) | data formatting | bytes 19922944 | tf_op jit(solution)/shard_map/kij,kjf->kif/dot_general | solution.py:43
  83.5 0.2 broadcast_in_dim.17
  83.7 21.0 %scatter_fusion = f32[33,128,128]{2,1,0:T(8,128)S(1)} fusion(f32[33,128,128]{2,1,0:T(8,128)S(1)} %broadcast_in_dim.17, s32[152]{0:T(256)S(1)} %bitcast.51, f32[152,128,128]{2,1,0:T(8,128)} %copy.12), kind=kCustom, calls=%fused_computation.3 | custom fusion | flops 2490368 | bytes 29885024 | tf_op jit(solution)/shard_map/scatter-add | solution.py:24
  104.7 1.5 slice.14
  106.2 0.0 reduce-scatter.3.cloned.1.call-update
  106.2 0.0 all-gather.2.cloned.1.call-start
  106.2 94.5 %reduce-scatter.3.cloned.1.call-done = f32[128,128]{1,0:T(8,128)} async-done(((f32[4096,128]{1,0:T(8,128)}), f32[128,128]{1,0:T(8,128)}) %reduce-scatter.3.cloned.1.call-update) | async-done | bytes 65552 | tf_op jit(solution)/shard_map/reduce_scatter | solution.py:47
  200.8 1.0 multiply_convert_fusion
  201.8 0.8 convolution_convert_fusion
  202.5 0.0 all-gather.2.cloned.1.call-update
  202.6 0.0 all-reduce.2.cloned.1.call-start
  202.6 1.7 fusion.10
  204.3 0.0 all-reduce.2.cloned.1.call-update
  204.3 0.2 reduce-scatter.5.cloned.1.call-start
  204.5 54.7 %all-gather.2.cloned.1.call-done = bf16[4096,128]{1,0:T(8,128)(2,1)} async-done(((bf16[128,128]{1,0:T(8,128)(2,1)}), bf16[4096,128]{1,0:T(8,128)(2,1)}) %all-gather.2.cloned.1.call-update) | async-done | bytes 1048592 | tf_op jit(solution)/shard_map/all_gather | solution.py:51
  259.3 8.9 %gather_fusion.1 = bf16[152,128,128]{2,1,0:T(8,128)(2,1)} fusion(bf16[32,128,128]{2,1,0:T(8,128)(2,1)} %bitcast.47, s32[1024]{0:T(1024)S(1)} %pad_clamp_fusion.1), kind=kCustom, calls=%fused_computation.1 | custom fusion | bytes 9962080 | tf_op jit(solution)/shard_map/gather | solution.py:53
  268.2 9.5 %fusion.7 = f32[152,128,128]{1,2,0:T(8,128)} fusion(bf16[152,128,128]{2,1,0:T(8,128)(2,1)} %gather_fusion.1, bf16[1,1,152,128,128]{4,3,2,1,0:T(8,128)(2,1)} %param.11), kind=kOutput, calls=%fused_computation.10 | convolution fusion | flops 637534208 | bytes 19922944 | tf_op jit(solution)/shard_map/kij,kif->kjf/dot_general | solution.py:54
  277.7 11.3 %copy.14 = f32[152,128,128]{2,1,0:T(8,128)} copy(f32[152,128,128]{1,2,0:T(8,128)} %fusion.7) | data formatting | bytes 19922944 | tf_op jit(solution)/shard_map/kij,kif->kjf/dot_general | solution.py:54
  289.0 0.1 broadcast_in_dim.16
  289.2 21.0 %scatter_fusion.1 = f32[17,128,128]{2,1,0:T(8,128)S(1)} fusion(f32[17,128,128]{2,1,0:T(8,128)S(1)} %broadcast_in_dim.16, s32[152]{0:T(256)S(1)} %bitcast.50, f32[152,128,128]{2,1,0:T(8,128)} %copy.14), kind=kCustom, calls=%fused_computation.4 | custom fusion | flops 2490368 | bytes 29885024 | tf_op jit(solution)/shard_map/scatter-add | solution.py:24
  310.1 1.0 slice.15
  311.2 0.0 reduce-scatter.5.cloned.1.call-update
  311.2 211.2 %all-reduce.2.cloned.1.call-done = f32[128,128]{1,0:T(8,128)} async-done(((f32[128,128]{1,0:T(8,128)}), f32[128,128]{1,0:T(8,128)}) %all-reduce.2.cloned.1.call-update) | async-done | bytes 65552 | tf_op jit(solution)/shard_map/psum | solution.py:52
  522.4 1.5 broadcast_multiply_fusion
  523.9 74.6 %reduce-scatter.5.cloned.1.call-done = f32[128,128]{1,0:T(8,128)} async-done(((f32[2048,128]{1,0:T(8,128)}), f32[128,128]{1,0:T(8,128)}) %reduce-scatter.5.cloned.1.call-update) | async-done | bytes 65552 | tf_op jit(solution)/shard_map/reduce_scatter | solution.py:60
  598.5 0.8 convert_element_type.19
  599.4 1.3 gather_fusion.2
  (11 shorter events, 0.1 us)
Async XLA Ops:
  7.2 193.6 %copy-start = (bf16[128,128]{1,0:T(8,128)(2,1)S(1)}, bf16[128,128]{1,0:T(8,128)(2,1)}, u32[]{:S(2)}) copy-start(bf16[128,128]{1,0:T(8,128)(2,1)} %param.9) | copy-start | bytes 98308
  7.2 193.6 %reduce-scatter.3.cloned.1.call-start = ((), (), s32[]{:S(2)}) async-start(), calls=%async_computation.2 | async-start | bytes 2162688 | tf_op jit(solution)/shard_map/reduce_scatter | solution.py:47
  104.7 96.1 %copy-start.1 = (bf16[128,128]{1,0:T(8,128)(2,1)S(1)}, bf16[128,128]{1,0:T(8,128)(2,1)}, u32[]{:S(2)}) copy-start(bf16[128,128]{1,0:T(8,128)(2,1)} %param.8) | copy-start | bytes 98308
  106.2 153.1 %all-gather.2.cloned.1.call-start = ((), (), s32[]{:S(2)}) async-start(), calls=%async_computation.3 | async-start | bytes 1081344 | tf_op jit(solution)/shard_map/all_gather | solution.py:51
  202.6 319.9 %all-reduce.2.cloned.1.call-start = ((), (), s32[]{:S(2)}) async-start(), calls=%async_computation.5 | async-start | bytes 131072 | tf_op jit(solution)/shard_map/psum | solution.py:52
  204.3 394.2 %reduce-scatter.5.cloned.1.call-start = ((), (), s32[]{:S(2)}) async-start(), calls=%async_computation.4 | async-start | bytes 1114112 | tf_op jit(solution)/shard_map/reduce_scatter | solution.py:60
  289.2 22.1 %copy-start.2 = (s32[1,128]{1,0:T(1,128)S(1)}, s32[1,128]{1,0:T(1,128)}, u32[]{:S(2)}) copy-start(s32[1,128]{1,0:T(1,128)} %param.13) | copy-start | bytes 1540
Sparse Core Ops, SparseCore 0:
  106.3 94.3 reduce-scatter.2
  204.5 54.7 all-gather.1
  264.8 257.5 all-reduce.1
  525.1 73.4 reduce-scatter.4
where the time goes:
time: 609 us; the launch traced here: 607 us
  waiting for transfers between devices  435 us (71%)
  other arithmetic  45 us (7%)
  blocking collectives  44.5 us (7%)
  local copies, waits for them, and re-layouts  43.5 us (7%)
  matrix products  24.3 us (4%)
  between operations  14.5 us (2%)
    psum x1, waiting for transfers between devices, shards(): lax.psum(weight_part, ('row', 'col')) * (1.0 / math.sqrt(total_nodes))  211 us
    reduce_scatter x1, waiting for transfers between devices, shards(): lax.psum_scatter(partial_value, 'col', scatter_dimension=0, tiled=True)  94.5 us
    reduce_scatter x1, waiting for transfers between devices, shards(): lax.psum_scatter(partial_back, 'row', scatter_dimension=0, tiled=True)  74.6 us
    all_gather x1, waiting for transfers between devices, shards(): grad_rows = lax.all_gather(grad_share, 'col', axis=0, tiled=True)  54.7 us
    all_gather x1, blocking collectives, shards(): column_source = lax.all_gather(features, 'row', axis=0, tiled=True)  44.5 us
    scatter-add x2, other arithmetic, block_sums(): summed = jax.ops.segment_sum(product, routed, num_segments=segments + 1)  41.9 us
  transfers between devices with their start and end apart: 4, of which 4 were waited for; matrix products, arithmetic and copies ran while one was open for 9% of the time, Pallas kernels for 0%

commit v1 on v0

--- a/solution.py
+++ b/solution.py
@@ -49,7 +49,9 @@
     grad_pre, grad_share = grad_step(agg_low, grad_out, weight)
     weight_part = jnp.dot(agg_low.T, grad_pre, preferred_element_type=jnp.float32)
     grad_rows = lax.all_gather(grad_share, "col", axis=0, tiled=True)
-    weight_grad = lax.psum(weight_part, ("row", "col")) * (1.0 / math.sqrt(total_nodes))
+    weight_grad = jnp.sum(lax.all_gather(weight_part, ("row", "col")), axis=0) * (
+        1.0 / math.sqrt(total_nodes)
+    )
     picked_back = grad_rows.reshape(row_count, BLOCK, hidden)[block_row]
     product_back = jnp.einsum(
         "kij,kif->kjf", values, picked_back, preferred_element_type=jnp.float32

time: 609 us -> 1260 us (2.07)
  the two profiles are of different devices: /device:TPU:4 before, /device:TPU:24 now
where the time goes in v1:
time: 1260 us
  waiting for transfers between devices  1080 us (86%)
  other arithmetic  57.2 us (5%)
  local copies, waits for them, and re-layouts  43.5 us (3%)
  blocking collectives  40.9 us (3%)
  matrix products  23.5 us (2%)
  between operations  14.5 us (1%)
    all_gather x1, waiting for transfers between devices, shards(): lax.all_gather(weight_part, ('row', 'col'))  852 us
    reduce_scatter x1, waiting for transfers between devices, shards(): lax.psum_scatter(partial_value, 'col', scatter_dimension=0, tiled=True)  97 us
    reduce_scatter x1, waiting for transfers between devices, shards(): lax.psum_scatter(partial_back, 'row', scatter_dimension=0, tiled=True)  72.5 us
    all_gather x1, waiting for transfers between devices, shards(): grad_rows = lax.all_gather(grad_share, 'col', axis=0, tiled=True)  56.5 us
    scatter-add x2, other arithmetic, block_sums(): summed = jax.ops.segment_sum(product, routed, num_segments=segments + 1)  41.9 us
    all_gather x1, blocking collectives, shards(): column_source = lax.all_gather(features, 'row', axis=0, tiled=True)  40.9 us
  transfers between devices with their start and end apart: 4, of which 4 were waited for; matrix products, arithmetic and copies ran while one was open for 0% of the time, Pallas kernels for 0%

profile of v1, /device:TPU:24, one launch (start us, length us, event | category | flops | bytes accessed | tf_op | source)
XLA Modules:
  0.0 1258.4 jit_solution(2482154340775462576)
XLA Ops:
  7.2 0.0 reduce-scatter.3.cloned.1.call-start
  7.2 0.7 compare_select_fusion
  8.6 40.9 %all_gather.12 = bf16[2048,128]{1,0:T(8,128)(2,1)S(1)} all-gather(bf16[128,128]{1,0:T(8,128)(2,1)} %param.7), channel_id=1, replica_groups=mesh['row'=16,'col'=32] {'row'}, dimensions={0}, use_global_device_ids=true | all-gather | bytes 557056 | tf_op jit(solution)/shard_map/all_gather | solution.py:41
  49.5 7.7 gather_fusion
  57.2 11.4 fusion.4
  68.6 11.3 copy.12
  79.9 0.2 broadcast_in_dim.17
  80.1 20.9 %scatter_fusion = f32[33,128,128]{2,1,0:T(8,128)S(1)} fusion(f32[33,128,128]{2,1,0:T(8,128)S(1)} %broadcast_in_dim.17, s32[152]{0:T(256)S(1)} %bitcast.53, f32[152,128,128]{2,1,0:T(8,128)} %copy.12), kind=kCustom, calls=%fused_computation.3 | custom fusion | flops 2490368 | bytes 29885024 | tf_op jit(solution)/shard_map/scatter-add | solution.py:24
  101.1 1.5 slice.14
  102.6 0.0 all-gather.4.cloned.1.call-start
  102.6 97.0 %reduce-scatter.3.cloned.1.call-done = f32[128,128]{1,0:T(8,128)} async-done(((f32[4096,128]{1,0:T(8,128)}), f32[128,128]{1,0:T(8,128)}) %reduce-scatter.3.cloned.1.call-update) | async-done | bytes 65552 | tf_op jit(solution)/shard_map/reduce_scatter | solution.py:47
  199.6 1.0 multiply_convert_fusion
  200.6 0.8 convolution_convert_fusion
  201.4 0.0 all-gather.4.cloned.1.call-update
  201.4 0.2 reduce-scatter.5.cloned.1.call-start
  201.7 56.5 %all-gather.4.cloned.1.call-done = bf16[4096,128]{1,0:T(8,128)(2,1)} async-done(((bf16[128,128]{1,0:T(8,128)(2,1)}), bf16[4096,128]{1,0:T(8,128)(2,1)}) %all-gather.4.cloned.1.call-update) | async-done | bytes 1048592 | tf_op jit(solution)/shard_map/all_gather | solution.py:51
  258.2 8.9 gather_fusion.1
  267.1 9.5 fusion.7
  276.6 11.3 copy.14
  288.0 0.1 broadcast_in_dim.16
  288.1 20.9 %scatter_fusion.1 = f32[17,128,128]{2,1,0:T(8,128)S(1)} fusion(f32[17,128,128]{2,1,0:T(8,128)S(1)} %broadcast_in_dim.16, s32[152]{0:T(256)S(1)} %bitcast.52, f32[152,128,128]{2,1,0:T(8,128)} %copy.14), kind=kCustom, calls=%fused_computation.4 | custom fusion | flops 2490368 | bytes 29885024 | tf_op jit(solution)/shard_map/scatter-add | solution.py:24
  309.0 1.0 slice.15
  310.1 0.0 reduce-scatter.5.cloned.1.call-update
  310.1 0.0 all-gather.6.cloned.1.call-start
  310.2 0.8 fusion.10
  311.0 0.0 all-gather.6.cloned.1.call-update
  311.0 72.5 %reduce-scatter.5.cloned.1.call-done = f32[128,128]{1,0:T(8,128)} async-done(((f32[2048,128]{1,0:T(8,128)}), f32[128,128]{1,0:T(8,128)}) %reduce-scatter.5.cloned.1.call-update) | async-done | bytes 65552 | tf_op jit(solution)/shard_map/reduce_scatter | solution.py:62
  383.5 0.8 convert_element_type.19
  384.4 1.3 gather_fusion.2
  385.7 852.4 %all-gather.6.cloned.1.call-done = f32[65536,128]{1,0:T(8,128)} async-done(((f32[128,128]{1,0:T(8,128)}), f32[65536,128]{1,0:T(8,128)}) %all-gather.6.cloned.1.call-update) | async-done | bytes 33554448 | tf_op jit(solution)/shard_map/all_gather | solution.py:52
  1238.1 13.1 %reduce_sum.9 = f32[128,128]{1,0:T(8,128)S(1)} reduce(f32[512,128,128]{2,1,0:T(8,128)} %bitcast.48, f32[]{:T(128)} %constant.18.clone.1), dimensions={0}, to_apply=%region_4.5 | reduce | flops 8372224 | bytes 33619972 | tf_op jit(solution)/shard_map/reduce_sum | solution.py:52
  1251.2 0.6 broadcast_multiply_fusion
  (16 shorter events, 0.1 us)
Async XLA Ops:
  7.2 192.4 %copy-start = (bf16[128,128]{1,0:T(8,128)(2,1)S(1)}, bf16[128,128]{1,0:T(8,128)(2,1)}, u32[]{:S(2)}) copy-start(bf16[128,128]{1,0:T(8,128)(2,1)} %param.9) | copy-start | bytes 98308
  7.2 192.4 %reduce-scatter.3.cloned.1.call-start = ((), (), s32[]{:S(2)}) async-start(), calls=%async_computation.2 | async-start | bytes 2162688 | tf_op jit(solution)/shard_map/reduce_scatter | solution.py:47
  101.1 98.5 %copy-start.3 = (bf16[128,128]{1,0:T(8,128)(2,1)S(1)}, bf16[128,128]{1,0:T(8,128)(2,1)}, u32[]{:S(2)}) copy-start(bf16[128,128]{1,0:T(8,128)(2,1)} %param.8) | copy-start | bytes 98308
  102.6 155.6 %all-gather.4.cloned.1.call-start = ((), (), s32[]{:S(2)}) async-start(), calls=%async_computation.3 | async-start | bytes 1081344 | tf_op jit(solution)/shard_map/all_gather | solution.py:51
  201.4 182.1 %reduce-scatter.5.cloned.1.call-start = ((), (), s32[]{:S(2)}) async-start(), calls=%async_computation.4 | async-start | bytes 1114112 | tf_op jit(solution)/shard_map/reduce_scatter | solution.py:62
  288.1 22.1 %copy-start.2 = (f32[128,128]{1,0:T(8,128)S(1)}, f32[128,128]{1,0:T(8,128)}, u32[]{:S(2)}) copy-start(f32[128,128]{1,0:T(8,128)} %reduce-scatter.3.cloned.1.call-done) | copy-start | bytes 196612
  288.1 22.9 %copy-start.4 = (s32[1,128]{1,0:T(1,128)S(1)}, s32[1,128]{1,0:T(1,128)}, u32[]{:S(2)}) copy-start(s32[1,128]{1,0:T(1,128)} %param.13) | copy-start | bytes 1540
  310.1 928.0 %all-gather.6.cloned.1.call-start = ((), (), s32[]{:S(2)}) async-start(), calls=%async_computation.5 | async-start | bytes 33619968 | tf_op jit(solution)/shard_map/all_gather | solution.py:52
  1238.1 13.7 %copy-start.1 = (bf16[128,128]{1,0:T(8,128)(2,1)S(1)}, bf16[128,128]{1,0:T(8,128)(2,1)}, u32[]{:S(2)}) copy-start(bf16[128,128]{1,0:T(8,128)(2,1)} %param.9) | copy-start | bytes 98308
Sparse Core Ops, SparseCore 0:
  102.7 96.8 reduce-scatter.2
  203.3 54.8 all-gather.3
  310.2 73.2 reduce-scatter.4
  386.2 851.8 all-gather.5
